TPU v7x, 32 devices: a whole 2x2x4 slice. The times are simulated.
32 devices in a mesh: dom: 4 (over y, x), sep: 8 (over z, core).
Axes of the slice: x: 2, y: 2, z: 4, core: 2. Of those that a mesh axis runs over, the one named last changes fastest.
Arguments:
- rhs_leaf: bfloat16 [4, 4096, 1536], P('dom', 'sep'), may hold values from -6 to 6
- rhs_middle: bfloat16 [4, 4096, 768], P('dom', 'sep'), may hold values from -6 to 6
- rhs_top: bfloat16 [4, 4096, 384], P('dom', 'sep'), may hold values from -6 to 6
- update_leaf: bfloat16 [4, 4096, 256], P('dom', 'sep'), may hold values from -0.375 to 0.375
- couple_leaf: bfloat16 [4, 4096, 256], P('dom', 'sep'), may hold values from -0.09375 to 0.09375
- update_middle: bfloat16 [4, 4096, 256], P('dom', 'sep'), may hold values from -0.375 to 0.375, as said below
- couple_middle: bfloat16 [4, 4096, 256], P('dom', 'sep'), may hold values from -0.09375 to 0.09375, as said below
- pivot_leaf: float32 [4, 4096], P('dom', 'sep'), may hold values from 2.2 to 4
- pivot_middle: float32 [2, 4096], P(None, 'sep'), may hold values from 2.2 to 4
- pivot_top: float32 [1, 4096], P(None, 'sep'), may hold values from 2.2 to 4
- front_rows: int32 [4, 8], P('dom', 'sep'), may hold values from 128 to 512, as said below
- rank_leaf: int32 [4], P('dom'), may hold values from 64 to 256, as said below
- rank_middle: int32 [2], replicated, may hold values from 64 to 256, as said below
Outputs:
- top_values: float32 [4, 4096, 384], P('dom', 'sep')
Inputs may be any that keep to these rules, and one draw needn't show every extreme that they name: `front_rows`: in every draw some front has all 512 rows of some row block live. `rank_leaf`: some leaf front has rank 256 in every draw. `rank_middle`: some middle front has rank 256 in every draw. `update_middle`: rows 2g and 2g+1 are equal; entries lie within plus or minus 6 / sqrt(256). `couple_middle`: rows 2g and 2g+1 are equal; entries lie within plus or minus 6 / sqrt(4096).
All inputs are finite; a program needn't handle non-finite values.
Results may differ from a plain program's by a relative error of at most 0.0018.
Values may be sent and summed in bfloat16 or wider, within the bound.
A program may use at most 64 MiB of HBM per device.

v0:
```python
import jax
import jax.numpy as jnp
from jax import lax
from jax.sharding import PartitionSpec as P


def extended(cells, sides, width):
    for axis, dim in sides:
        count = lax.axis_size(axis)
        ends = count - 1
        head = lax.slice_in_dim(cells, 0, width, axis=dim)
        tail = lax.slice_in_dim(cells, cells.shape[dim] - width, cells.shape[dim], axis=dim)
        cells = jnp.concatenate(
            [
                lax.ppermute(tail, axis, [(i, (i + 1) % count) for i in range(ends)]),
                cells,
                lax.ppermute(head, axis, [((i + 1) % count, i) for i in range(ends)]),
            ],
            axis=dim,
        )
    return cells


def from_partner(value, axis, bit):
    mask = 2**bit
    pairs = [(source, source ^ mask) for source in range(lax.axis_size(axis))]
    return lax.ppermute(value, axis, pairs)


def solve_rows(right_side, pivots, row_mask):
    scaled = row_mask[:, None] * right_side / pivots[:, None]
    padded = extended(scaled, (("sep", 0),), 1)
    beside = padded[:-2] + padded[2:]
    return scaled + row_mask[:, None] * beside / pivots[:, None]


def coefficients(factor, values, rank):
    partial_sum = lax.dot_general(
        factor, values, (((0,), (0,)), ((), ())), preferred_element_type=jnp.float32
    )
    rank_keep = (jnp.arange(factor.shape[1]) < rank).astype(jnp.float32)
    kept_sum = partial_sum * rank_keep[:, None]
    return lax.psum(kept_sum, "sep").astype(jnp.bfloat16)


def combine(factor, coef_block, keep_half, swap_bit):
    half_width = coef_block.shape[1] // 2
    own_half = lax.dynamic_slice_in_dim(coef_block, keep_half * half_width, half_width, 1)
    other_half = lax.dynamic_slice_in_dim(coef_block, (1 - keep_half) * half_width, half_width, 1)
    mine_term = jnp.dot(factor, own_half, preferred_element_type=jnp.float32)
    outgoing = jnp.dot(factor, other_half, preferred_element_type=jnp.float32)
    return mine_term + from_partner(outgoing, "dom", swap_bit)


def shards(
    rhs_leaf,
    rhs_middle,
    rhs_top,
    update_leaf,
    couple_leaf,
    update_middle,
    couple_middle,
    pivot_leaf,
    pivot_middle,
    pivot_top,
    front_rows,
    rank_leaf,
    rank_middle,
):
    front = lax.axis_index("dom")
    middle = front // 2
    top_front = front // 4
    row_count = rhs_leaf.shape[1]
    live = (jnp.arange(row_count) < front_rows[0, 0]).astype(jnp.float32)
    every_row = jnp.ones((row_count,), jnp.float32)
    leaf_values = solve_rows(rhs_leaf[0].astype(jnp.float32), pivot_leaf[0], live).astype(
        jnp.bfloat16
    )
    leaf_coef = coefficients(couple_leaf[0], leaf_values, rank_leaf[0])
    middle_rhs = rhs_middle[0].astype(jnp.float32) - combine(
        update_leaf[0], leaf_coef, front % 2, 0
    )
    middle_pivot = lax.dynamic_index_in_dim(pivot_middle, middle, 0, keepdims=False)
    middle_values = solve_rows(middle_rhs, middle_pivot, every_row).astype(jnp.bfloat16)
    middle_rank = lax.dynamic_index_in_dim(rank_middle, middle, 0, keepdims=False)
    middle_coef = coefficients(couple_middle[0], middle_values, middle_rank)
    top_rhs = rhs_top[0].astype(jnp.float32) - combine(update_middle[0], middle_coef, middle % 2, 1)
    top_pivot = lax.dynamic_index_in_dim(pivot_top, top_front, 0, keepdims=False)
    return solve_rows(top_rhs, top_pivot, every_row)[None]


def solution(mesh):
    return jax.shard_map(
        shards,
        mesh=mesh,
        in_specs=(
            P("dom", "sep", None),
            P("dom", "sep", None),
            P("dom", "sep", None),
            P("dom", "sep", None),
            P("dom", "sep", None),
            P("dom", "sep", None),
            P("dom", "sep", None),
            P("dom", "sep"),
            P(None, "sep"),
            P(None, "sep"),
            P("dom", "sep"),
            P("dom"),
            P(),
        ),
        out_specs=P("dom", "sep", None),
        check_vma=False,
    )
```

profile of v0, /device:TPU:0, one launch (start us, length us, event | category | flops | bytes accessed | tf_op | source)
XLA Modules:
  0.0 177.0 jit_solution(2106468252717800136)
XLA Ops:
  0.7 1.8 %fusion.4 = f32[512,1536]{1,0:T(8,128)S(1)} fusion(bf16[1,512,1536]{2,1,0:T(8,128)(2,1)} %param.13, f32[512]{0:T(512)} %bitcast.55, f32[512]{0:T(512)S(1)} %fusion.32), kind=kLoop, calls=%fused_computation.7 | loop fusion | flops 2359296 | bytes 4722688 | tf_op jit(solution)/shard_map/div | solution.py:31
  2.5 1.3 collective-permute-start.1
  3.8 3.0 %collective-permute-start = (f32[1,1536]{1,0:T(1,128)S(1)}, f32[1,1536]{1,0:T(1,128)S(1)}, u32[]{:S(2)}, u32[]{:S(2)}) collective-permute-start(f32[1,1536]{1,0:T(1,128)S(1)} %get-tuple-element.5), channel_id=1, source_target_pairs={{0,1},{1,2},{2,3},{3,4},{4,5},{5,6},{6,7},{8,9},{9,10},{10,11},{11... | collective-permute-start | bytes 18440 | tf_op jit(solution)/shard_map/ppermute | solution.py:15
  7.7 3.4 %fusion.6 = f32[256,1536]{0,1:T(8,128)} fusion(f32[512,1536]{1,0:T(8,128)S(1)} %fusion.4, f32[1,1536]{1,0:T(1,128)S(1)} %collective-permute-done.1, f32[1,1536]{1,0:T(1,128)S(1)} %collective-permute-done, f32[512]{0:T(512)S(1)} %bitcast.56, f32[512]{0:T(512)S(1)} %fusion.32, f32[256]{0:T(256)S(1)} %compare_convert_fusion.1, bf16[1,512,256]{2,1,0:T(8,128)(2,1)} %param.17), kind=kOutput, calls=%fused_computation.10 | convolution fusion | flops 408551424 | bytes 4998144 | tf_op jit(solution)/shard_map/dot_general | solution.py:38
  11.1 63.0 %all-reduce.2 = bf16[256,1536]{0,1:T(8,128)(2,1)S(1)} all-reduce(f32[256,1536]{0,1:T(8,128)} %fusion.6), channel_id=1, replica_groups=mesh['dom'=4,'sep'=8] {'sep'}, use_global_device_ids=true, to_apply=%region_0.1 | all-reduce | flops 393216 | bytes 2359296 | tf_op jit(solution)/shard_map/psum | solution.py:43
  74.2 0.4 convolution_bitcast_fusion
  74.6 1.6 collective-permute-start.2
  76.2 0.6 dynamic_slice.25
  76.8 31.5 %collective-permute-done.2 = f32[512,768]{1,0:T(8,128)} collective-permute-done((f32[512,768]{1,0:T(8,128)S(1)}, f32[512,768]{1,0:T(8,128)}, u32[]{:S(2)}, u32[]{:S(2)}) %collective-permute-start.2) | collective-permute-done | bytes 1572896 | tf_op jit(solution)/shard_map/ppermute | solution.py:27
  108.3 1.8 %fusion.10 = f32[512,768]{1,0:T(8,128)S(1)} fusion(f32[512,768]{1,0:T(8,128)} %collective-permute-done.2, bf16[1,512,768]{2,1,0:T(8,128)(2,1)S(1)} %copy-done.6, f32[512]{0:T(512)S(1)} %bitcast.59, bf16[256,1536]{0,1:T(8,128)(2,1)S(1)} %all-reduce.2, s32[]{:T(128)S(6)} %select_n.37, bf16[1,512,256]{2,1,0:T(8,128)(2,1)S(1)} %copy-done), kind=kOutput, calls=%fused_computation.17 | convolution fusion | flops 202899456 | bytes 4589572 | tf_op jit(solution)/shard_map/dot_general | solution.py:50
  110.1 1.3 collective-permute-start.4
  111.4 3.0 %collective-permute-start.3 = (f32[1,768]{1,0:T(1,128)S(1)}, f32[1,768]{1,0:T(1,128)S(1)}, u32[]{:S(2)}, u32[]{:S(2)}) collective-permute-start(f32[1,768]{1,0:T(1,128)S(1)} %get-tuple-element.7), channel_id=1, source_target_pairs={{0,1},{1,2},{2,3},{3,4},{4,5},{5,6},{6,7},{8,9},{9,10},{10,11},{11... | collective-permute-start | bytes 9224 | tf_op jit(solution)/shard_map/ppermute | solution.py:15
  114.5 0.7 compare_convert_fusion
  115.3 1.6 fusion.16
  116.9 36.5 %all-reduce.3 = bf16[256,768]{0,1:T(8,128)(2,1)S(1)} all-reduce(f32[256,768]{0,1:T(8,128)S(1)} %fusion.16), channel_id=1, replica_groups=mesh['dom'=4,'sep'=8] {'sep'}, use_global_device_ids=true, to_apply=%region_1.2 | all-reduce | flops 196608 | bytes 1179648 | tf_op jit(solution)/shard_map/psum | solution.py:43
  153.4 0.3 convolution_bitcast_fusion.1
  153.7 1.6 collective-permute-start.5
  155.5 14.0 %collective-permute-done.5 = f32[512,384]{0,1:T(8,128)S(1)} collective-permute-done((f32[512,384]{0,1:T(8,128)S(1)}, f32[512,384]{0,1:T(8,128)S(1)}, u32[]{:S(2)}, u32[]{:S(2)}) %collective-permute-start.5) | collective-permute-done | bytes 786464 | tf_op jit(solution)/shard_map/ppermute | solution.py:27
  169.5 0.3 fusion.15
  169.9 1.3 collective-permute-start.7
  171.2 3.0 %collective-permute-start.6 = (f32[1,384]{0,1:T(8,128)S(1)}, f32[1,384]{0,1:T(8,128)S(1)}, u32[]{:S(2)}, u32[]{:S(2)}) collective-permute-start(f32[1,384]{0,1:T(8,128)S(1)} %get-tuple-element.9), channel_id=1, source_target_pairs={{0,1},{1,2},{2,3},{3,4},{4,5},{5,6},{6,7},{8,9},{9,10},{10,11},{11... | collective-permute-start | bytes 4616 | tf_op jit(solution)/shard_map/ppermute | solution.py:15
  174.3 1.0 collective-permute-done.6
  175.3 0.5 fusion.20
  175.8 1.1 copy.16
  (28 shorter events, 0.6 us)
Async XLA Ops:
  0.0 74.2 %copy-start = (bf16[1,512,256]{2,1,0:T(8,128)(2,1)S(1)}, bf16[1,512,256]{2,1,0:T(8,128)(2,1)}, u32[]{:S(2)}) copy-start(bf16[1,512,256]{2,1,0:T(8,128)(2,1)} %param.16) | copy-start | bytes 786436
  0.7 7.0 %copy-start.3 = (f32[1,512]{1,0:T(1,128)S(1)}, f32[1,512]{1,0:T(1,128)}, u32[]{:S(2)}) copy-start(f32[1,512]{1,0:T(1,128)} %param.20) | copy-start | bytes 6148
  2.5 5.0 %collective-permute-start.1 = (f32[1,1536]{1,0:T(1,128)S(1)}, f32[1,1536]{1,0:T(1,128)S(1)}, u32[]{:S(2)}, u32[]{:S(2)}) collective-permute-start(f32[1,1536]{1,0:T(1,128)S(1)} %get-tuple-element.6), channel_id=1, source_target_pairs={{1,0},{2,1},{3,2},{4,3},{5,4},{6,5},{7,6},{9,8},{10,9},{11,10},{12... | collective-permute-start | bytes 18440 | tf_op jit(solution)/shard_map/ppermute | solution.py:17
  3.8 3.8 %collective-permute-start = (f32[1,1536]{1,0:T(1,128)S(1)}, f32[1,1536]{1,0:T(1,128)S(1)}, u32[]{:S(2)}, u32[]{:S(2)}) collective-permute-start(f32[1,1536]{1,0:T(1,128)S(1)} %get-tuple-element.5), channel_id=1, source_target_pairs={{0,1},{1,2},{2,3},{3,4},{4,5},{5,6},{6,7},{8,9},{9,10},{10,11},{11... | collective-permute-start | bytes 18440 | tf_op jit(solution)/shard_map/ppermute | solution.py:15
  74.2 2.0 %copy-start.7 = (s32[2]{0:T(128)S(1)}, s32[2]{0:T(128)}, u32[]{:S(2)}) copy-start(s32[2]{0:T(128)} %param.25) | copy-start | bytes 28
  74.2 2.6 %copy-start.5 = (f32[2,512]{1,0:T(2,128)S(1)}, f32[2,512]{1,0:T(2,128)}, u32[]{:S(2)}) copy-start(f32[2,512]{1,0:T(2,128)} %param.21) | copy-start | bytes 12292
  74.2 34.1 %copy-start.6 = (bf16[1,512,768]{2,1,0:T(8,128)(2,1)S(1)}, bf16[1,512,768]{2,1,0:T(8,128)(2,1)}, u32[]{:S(2)}) copy-start(bf16[1,512,768]{2,1,0:T(8,128)(2,1)} %param.14) | copy-start | bytes 2359300
  74.6 33.6 %collective-permute-start.2 = (f32[512,768]{1,0:T(8,128)S(1)}, f32[512,768]{1,0:T(8,128)}, u32[]{:S(2)}, u32[]{:S(2)}) collective-permute-start(f32[512,768]{1,0:T(8,128)S(1)} %convolution_bitcast_fusion), channel_id=1, source_target_pairs={{0,8},{8,0},{16,24},{24,16},{1,9},{9,1},{17,25},{25,17},{2,10},{10... | collective-permute-start | bytes 4718600 | tf_op jit(solution)/shard_map/ppermute | solution.py:27
  110.1 5.0 %collective-permute-start.4 = (f32[1,768]{1,0:T(1,128)S(1)}, f32[1,768]{1,0:T(1,128)S(1)}, u32[]{:S(2)}, u32[]{:S(2)}) collective-permute-start(f32[1,768]{1,0:T(1,128)S(1)} %get-tuple-element.8), channel_id=1, source_target_pairs={{1,0},{2,1},{3,2},{4,3},{5,4},{6,5},{7,6},{9,8},{10,9},{11,10},{12... | collective-permute-start | bytes 9224 | tf_op jit(solution)/shard_map/ppermute | solution.py:17
  111.4 3.8 %collective-permute-start.3 = (f32[1,768]{1,0:T(1,128)S(1)}, f32[1,768]{1,0:T(1,128)S(1)}, u32[]{:S(2)}, u32[]{:S(2)}) collective-permute-start(f32[1,768]{1,0:T(1,128)S(1)} %get-tuple-element.7), channel_id=1, source_target_pairs={{0,1},{1,2},{2,3},{3,4},{4,5},{5,6},{6,7},{8,9},{9,10},{10,11},{11... | collective-permute-start | bytes 9224 | tf_op jit(solution)/shard_map/ppermute | solution.py:15
  115.2 38.2 %copy-start.2 = (bf16[1,512,256]{2,1,0:T(8,128)(2,1)S(1)}, bf16[1,512,256]{2,1,0:T(8,128)(2,1)}, u32[]{:S(2)}) copy-start(bf16[1,512,256]{2,1,0:T(8,128)(2,1)} %param.18) | copy-start | bytes 786436
  116.9 38.4 %copy-start.1 = (bf16[1,512,384]{2,1,0:T(8,128)(2,1)S(1)}, bf16[1,512,384]{2,1,0:T(8,128)(2,1)}, u32[]{:S(2)}) copy-start(bf16[1,512,384]{2,1,0:T(8,128)(2,1)} %param.15) | copy-start | bytes 1179652
  116.9 52.6 %copy-start.4 = (f32[1,512]{1,0:T(1,128)S(1)}, f32[1,512]{1,0:T(1,128)}, u32[]{:S(2)}) copy-start(f32[1,512]{1,0:T(1,128)} %param.22) | copy-start | bytes 6148
  153.7 15.8 %collective-permute-start.5 = (f32[512,384]{0,1:T(8,128)S(1)}, f32[512,384]{0,1:T(8,128)S(1)}, u32[]{:S(2)}, u32[]{:S(2)}) collective-permute-start(f32[512,384]{0,1:T(8,128)S(1)} %convolution_bitcast_fusion.1), channel_id=1, source_target_pairs={{0,16},{8,24},{16,0},{24,8},{1,17},{9,25},{17,1},{25,9},{2,18},{10... | collective-permute-start | bytes 2359304 | tf_op jit(solution)/shard_map/ppermute | solution.py:27
  169.9 4.4 %collective-permute-start.7 = (f32[1,384]{0,1:T(8,128)S(1)}, f32[1,384]{0,1:T(8,128)S(1)}, u32[]{:S(2)}, u32[]{:S(2)}) collective-permute-start(f32[1,384]{0,1:T(8,128)S(1)} %get-tuple-element.10), channel_id=1, source_target_pairs={{1,0},{2,1},{3,2},{4,3},{5,4},{6,5},{7,6},{9,8},{10,9},{11,10},{12... | collective-permute-start | bytes 4616 | tf_op jit(solution)/shard_map/ppermute | solution.py:17
  171.2 4.1 %collective-permute-start.6 = (f32[1,384]{0,1:T(8,128)S(1)}, f32[1,384]{0,1:T(8,128)S(1)}, u32[]{:S(2)}, u32[]{:S(2)}) collective-permute-start(f32[1,384]{0,1:T(8,128)S(1)} %get-tuple-element.9), channel_id=1, source_target_pairs={{0,1},{1,2},{2,3},{3,4},{4,5},{5,6},{6,7},{8,9},{9,10},{10,11},{11... | collective-permute-start | bytes 4616 | tf_op jit(solution)/shard_map/ppermute | solution.py:15
where the time goes:
time: 180 us; the launch traced here: 177 us
  blocking collectives  99.5 us (55%)
  waiting for transfers between devices  46.7 us (26%)
  starting transfers between devices  16.1 us (9%)
  matrix products  7.85 us (4%)
  other arithmetic  2.97 us (2%)
  local copies, waits for them, and re-layouts  2.12 us (1%)
    psum x2, blocking collectives, coefficients(): return lax.psum(kept_sum, 'sep').astype(jnp.bfloat16)  99.5 us
    ppermute x2, waiting for transfers between devices, from_partner(): return lax.ppermute(value, axis, pairs)  45.5 us
    ppermute x3, starting transfers between devices, extended(): lax.ppermute(tail, axis, [(i, (i + 1) % count) for i in range(ends)])  9.1 us
    dot_general x2, matrix products, coefficients(): lax.dot_general(factor, values, (((0,), (0,)), ((), ())), preferred_eleme...  5.01 us
    ppermute x3, starting transfers between devices, extended(): lax.ppermute(head, axis, [((i + 1) % count, i) for i in range(ends)])  3.88 us
  transfers between devices with their start and end apart: 8, of which 5 were waited for; matrix products, arithmetic and copies ran while one was open for 1% of the time, Pallas kernels for 0%

commit v1 on v0

v1 whole, which is shorter than its diff:
```python
import functools

import jax
import jax.numpy as jnp
from jax import lax
from jax.experimental import pallas as pl
from jax.experimental.pallas import tpu as pltpu
from jax.sharding import PartitionSpec as P

MESH = pl.DeviceIdType.MESH
F32 = jnp.float32
BF16 = jnp.bfloat16
CW = 128
HOP = 3
LAG = 2
LAND = 2


def flipped(value, bit):
    return value + bit - 2 * bit * (lax.rem(value // bit, 2))


def spread(row, height):
    return jnp.broadcast_to(row, (height, row.shape[1])).T


def kernel(
    n_sep,
    rhs_leaf, rhs_middle, rhs_top, update_leaf, couple_leaf, update_middle, couple_middle,
    pivot_leaf, pivot_middle, pivot_top, front_rows, rank_leaf, rank_middle,
    out,
    leaf_v, middle_v, top_v, couple_v, factor_leaf, factor_middle,
    turned_leaf, turned_middle, weights,
    edge_send, edge_recv, row_send, row_recv,
    pair_send, pair_recv, own, leaf_lines, middle_lines, final_send,
    coef_leaf, coef_middle,
    load_sem, factor_send_sem, factor_recv_sem, edge_send_sem, edge_recv_sem,
    row_send_sem, row_recv_sem,
    pair_send_sem, pair_recv_sem, right_send_sem, left_send_sem, right_recv_sem, left_recv_sem,
    final_send_sem, coef_leaf_sem, coef_middle_sem,
):
    front = lax.axis_index("dom")
    sep = lax.axis_index("sep")
    n_z = n_sep // 2
    z = sep // 2
    core = lax.rem(sep, 2)
    side = lax.rem(front, 2)
    group = lax.rem(front // 2, 2)
    across = flipped(front, 1)
    over = flipped(front, 2)
    sibling = flipped(sep, 1)
    beside = sep - 1 + 2 * core
    has_beside = jnp.logical_and(beside >= 0, beside < n_sep)
    n_beside = has_beside.astype(jnp.int32)
    not_first = (z > 0).astype(jnp.int32)
    not_last = (z < n_z - 1).astype(jnp.int32)

    rows, width = leaf_v.shape
    half = width // 2
    quarter = width // 4
    rank = couple_v.shape[2]
    own_rank = rank // 2
    n_top = quarter // CW
    n_mid = 2 * n_top
    n_leaf = 2 * n_mid

    loads = [
        pltpu.make_async_copy(rhs_leaf.at[0], leaf_v, load_sem.at[0]),
        pltpu.make_async_copy(couple_leaf.at[0], couple_v.at[0], load_sem.at[1]),
        pltpu.make_async_copy(
            update_leaf.at[0], factor_leaf.at[side, pl.ds(0, rows)], load_sem.at[2]
        ),
        pltpu.make_async_copy(
            update_middle.at[0], factor_middle.at[group, pl.ds(0, rows)], load_sem.at[3]
        ),
        pltpu.make_async_copy(rhs_middle.at[0], middle_v, load_sem.at[4]),
        pltpu.make_async_copy(rhs_top.at[0], top_v, load_sem.at[5]),
        pltpu.make_async_copy(couple_middle.at[0], couple_v.at[1], load_sem.at[6]),
    ]
    for load in loads:
        load.start()

    barrier = pltpu.get_barrier_semaphore()

    def greet(dom_at, sep_at):
        pl.semaphore_signal(barrier, inc=1, device_id=(dom_at, sep_at), device_id_type=MESH)

    for dom_at in (front, across, over):
        greet(dom_at, sibling)
    for dom_at in (across, over):
        greet(dom_at, sep)

    @pl.when(has_beside)
    def _():
        for dom_at in (front, across, over):
            greet(dom_at, beside)

    @pl.when(z > 0)
    def _():
        greet(front, sep - 2)

    @pl.when(z < n_z - 1)
    def _():
        greet(front, sep + 2)

    @pl.when(sep == 0)
    def _():
        edge_recv[0] = jnp.zeros(edge_recv.shape[1:], F32)
        for slot in range(3):
            row_recv[slot, 0] = jnp.zeros(row_recv.shape[2:], F32)

    @pl.when(sep == n_sep - 1)
    def _():
        edge_recv[1] = jnp.zeros(edge_recv.shape[1:], F32)
        for slot in range(3):
            row_recv[slot, 1] = jnp.zeros(row_recv.shape[2:], F32)

    @pl.when(z == 0)
    def _():
        for lines in (leaf_lines, middle_lines):
            lines[2] = jnp.zeros(lines.shape[1:], lines.dtype)

    @pl.when(z == n_z - 1)
    def _():
        for lines in (leaf_lines, middle_lines):
            lines[3] = jnp.zeros(lines.shape[1:], lines.dtype)

    row_at = lax.broadcasted_iota(jnp.int32, (rows, CW), 0)
    live = (row_at < front_rows[0, 0]).astype(F32)
    weights[0] = live * (1.0 / spread(pivot_leaf[...], CW))
    weights[1] = 1.0 / spread(pivot_middle[pl.ds(front // 2, 1), :], CW)
    weights[2] = 1.0 / spread(pivot_top[pl.ds(front // 4, 1), :], CW)

    for load in loads[:6]:
        load.wait()

    ends = (rows - 16, 0)
    picks = (15, 0)
    for way in range(2):
        block = pl.ds(ends[way], 16)
        pick = slice(picks[way], picks[way] + 1)
        leaf_row = leaf_v[block, :].astype(F32)[pick]
        leaf_weight = weights[0, block, :][pick][:, :1]
        edge_send[way, :, :width] = leaf_row * leaf_weight
        edge_send[way, :, width : width + half] = middle_v[block, :].astype(F32)[pick]
        edge_send[way, :, width + half : width + half + quarter] = (
            top_v[block, :].astype(F32)[pick]
        )
        tail = width + half + quarter
        edge_send[way, :, tail : tail + CW] = weights[1, block, :][pick]
        edge_send[way, :, tail + CW : tail + 2 * CW] = weights[2, block, :][pick]
        row_send[way, :, :rank] = factor_leaf[side, block, :].astype(F32)[pick]
        row_send[way, :, rank:] = factor_middle[group, block, :].astype(F32)[pick]

    pl.semaphore_wait(barrier, 5 + 3 * n_beside + not_first + not_last)

    def edge_copies(way, target):
        copies = [
            pltpu.make_async_remote_copy(
                edge_send.at[way], edge_recv.at[way], edge_send_sem.at[way],
                edge_recv_sem.at[way], device_id=(front, target), device_id_type=MESH,
            )
        ]
        for slot, dom_at in enumerate((front, across, over)):
            copies.append(
                pltpu.make_async_remote_copy(
                    row_send.at[way], row_recv.at[slot, way], row_send_sem.at[slot, way],
                    row_recv_sem.at[slot, way], device_id=(dom_at, target), device_id_type=MESH,
                )
            )
        return copies

    to_next = edge_copies(0, sep + 1)
    to_prev = edge_copies(1, sep - 1)

    @pl.when(sep < n_sep - 1)
    def _():
        for copy in to_next:
            copy.start()

    @pl.when(sep > 0)
    def _():
        for copy in to_prev:
            copy.start()

    factor_copies = [
        pltpu.make_async_remote_copy(
            factor_leaf.at[side, pl.ds(0, rows)], factor_leaf.at[side, pl.ds(0, rows)],
            factor_send_sem.at[0], factor_recv_sem.at[0],
            device_id=(across, sep), device_id_type=MESH,
        ),
        pltpu.make_async_remote_copy(
            factor_middle.at[group, pl.ds(0, rows)], factor_middle.at[group, pl.ds(0, rows)],
            factor_send_sem.at[1], factor_recv_sem.at[1],
            device_id=(over, sep), device_id_type=MESH,
        ),
    ]
    for copy in factor_copies:
        copy.start()

    def turn(which, turned):
        for part in range(2):
            at = pl.multiple_of(own_rank * (core if part == 0 else 1 - core), own_rank)
            turned[pl.ds(part * own_rank, own_rank), :] = couple_v[
                which, :, pl.ds(at, own_rank)
            ].T

    turn(0, turned_leaf)

    @pl.when(sep > 0)
    def _():
        to_next[0].wait_recv()

    @pl.when(sep < n_sep - 1)
    def _():
        to_prev[0].wait_recv()

    def solved(right_side, weight, before, after):
        scaled = right_side * weight
        up = jnp.where(row_at == 0, before, pltpu.roll(scaled, 1, 0))
        down = jnp.where(row_at == rows - 1, after, pltpu.roll(scaled, rows - 1, 0))
        return scaled + weight * (up + down)

    def place(i):
        here = lax.rem(i, 2)
        at_quarter = here * group + (1 - here) * (1 - group)
        return at_quarter * n_top + i // 2

    def to_device(src, dst, send_sem, recv_sem, dom_at, sep_at):
        return pltpu.make_async_remote_copy(
            src, dst, send_sem, recv_sem, device_id=(dom_at, sep_at), device_id_type=MESH
        )

    def pair_copy(slot):
        return to_device(
            pair_send.at[slot], pair_recv.at[slot], pair_send_sem.at[slot],
            pair_recv_sem.at[slot], front, sibling,
        )

    def right_copy(lines, first_slot, j):
        slot = first_slot + j
        return to_device(
            lines.at[0, j], lines.at[2, j], right_send_sem.at[slot],
            right_recv_sem.at[slot], front, sep + 2,
        )

    def left_copy(lines, first_slot, j):
        slot = first_slot + j
        return to_device(
            lines.at[1, j], lines.at[3, j], left_send_sem.at[slot],
            left_recv_sem.at[slot], front, sep - 2,
        )

    def final_copy(slot, coef, sem, child, i, dom_at, sep_at, lane):
        return to_device(
            final_send.at[slot],
            coef.at[child, i, pl.ds(pl.multiple_of(core * own_rank, own_rank), own_rank)],
            final_send_sem.at[slot, lax.rem(lane, 2)], sem.at[i, lane], dom_at, sep_at,
        )

    def start_pair(slot, turned, values):
        part = jnp.dot(turned[...], values, preferred_element_type=F32)
        own[slot] = part[:own_rank]
        pair_send[slot] = part[own_rank:]
        pair_copy(slot).start()

    def chain(t, count, base, first_slot, stride, lines, rank_now, coef, coef_sem, child, partner):
        def on(step, body):
            j = (step + stride * count) // stride - count
            hit = jnp.logical_and(lax.rem(step + stride * count, stride) == 0, True)

            @pl.when(jnp.logical_and(hit, jnp.logical_and(step >= 0, j < count)))
            def _():
                body(j)

        def add_pair(j):
            slot = first_slot + j
            pair_copy(slot).wait_recv()
            own[slot] += pair_recv[slot]

        def prefix(j):
            slot = first_slot + j

            @pl.when(z > 0)
            def _():
                right_copy(lines, first_slot, j).wait_recv()

            @pl.when(z < n_z - 1)
            def _():
                lines[0, j] = (own[slot] + lines[2, j].astype(F32)).astype(lines.dtype)
                right_copy(lines, first_slot, j).start()

        def suffix(j):
            slot = first_slot + j

            @pl.when(z < n_z - 1)
            def _():
                left_copy(lines, first_slot, j).wait_recv()

            @pl.when(z > 0)
            def _():
                lines[1, j] = (own[slot] + lines[3, j].astype(F32)).astype(lines.dtype)
                left_copy(lines, first_slot, j).start()

        def final(j):
            slot = first_slot + j
            total = own[slot] + lines[2, j].astype(F32) + lines[3, j].astype(F32)
            at = core * own_rank + lax.broadcasted_iota(jnp.int32, total.shape, 0)
            kept = jnp.where(at < rank_now, total, 0.0).astype(BF16)
            final_send[slot] = kept
            i = j // 2

            @pl.when(lax.rem(j, 2) == 1)
            def _():
                coef[child, i, pl.ds(pl.multiple_of(core * own_rank, own_rank), own_rank)] = kept
                final_copy(slot, coef, coef_sem, child, i, front, sibling, 0).start()

            @pl.when(lax.rem(j, 2) == 0)
            def _():
                final_copy(slot, coef, coef_sem, child, i, partner, sep, 1).start()
                final_copy(slot, coef, coef_sem, child, i, partner, sibling, 2).start()

        start = t - base
        on(start, add_pair)
        on(start - z * HOP, prefix)
        on(start - (n_z - 1 - z) * HOP, suffix)
        on(start - jnp.maximum(z, n_z - 1 - z) * HOP, final)

    def await_coef(coef, sem, child, i):
        block = coef.at[child, i, pl.ds(0, own_rank)]
        for lane in range(3):
            to_device(
                final_send.at[0], block, final_send_sem.at[0, 0], sem.at[i, lane], front, sibling
            ).wait_recv()

    def applied(factor, coef, i):
        return jnp.dot(factor[0], coef[0, i], preferred_element_type=F32) + jnp.dot(
            factor[1], coef[1, i], preferred_element_type=F32
        )

    def leaf_step(j):
        i = j // 2
        own_side = lax.rem(j, 2)
        at_side = own_side * side + (1 - own_side) * (1 - side)
        at = pl.multiple_of(at_side * half + place(i) * CW, CW)
        values = solved(
            leaf_v[:, pl.ds(at, CW)].astype(F32), weights[0],
            edge_recv[0, :, pl.ds(at, CW)], edge_recv[1, :, pl.ds(at, CW)],
        ).astype(BF16)
        start_pair(j, turned_leaf, values)

    tail = width + half + quarter

    def eliminated(right_v, offset, at, factor, coef, i, which):
        taken = applied(factor, coef, i)
        beyond = []
        for way in range(2):
            right = edge_recv[way, :, pl.ds(pl.multiple_of(offset + at, CW), CW)]
            weight = edge_recv[way, :, tail + (which - 1) * CW : tail + which * CW]
            beyond.append((right - taken[rows + way : rows + way + 1]) * weight)
        return solved(
            right_v[:, pl.ds(at, CW)].astype(F32) - taken[:rows], weights[which], *beyond
        )

    def middle_step(i):
        await_coef(coef_leaf, coef_leaf_sem, side, i)
        at = pl.multiple_of(place(i) * CW, CW)
        values = eliminated(middle_v, width, at, factor_leaf, coef_leaf, i, 1).astype(BF16)
        start_pair(n_leaf + i, turned_middle, values)

    def top_step(i):
        await_coef(coef_middle, coef_middle_sem, group, i)
        at = pl.multiple_of(i * CW, CW)
        out[0, :, pl.ds(at, CW)] = eliminated(
            top_v, width + half, at, factor_middle, coef_middle, i, 2
        )

    def ready():
        loads[6].wait()
        turn(1, turned_middle)

        @pl.when(sep > 0)
        def _():
            for copy in to_next[1:]:
                copy.wait_recv()

        @pl.when(sep < n_sep - 1)
        def _():
            for copy in to_prev[1:]:
                copy.wait_recv()

        for copy in factor_copies:
            copy.wait_recv()

        at_row = lax.broadcasted_iota(jnp.int32, (16, rank), 0)

        def edge_tile(slot, lanes):
            before = row_recv[slot, 0, :, lanes]
            after = row_recv[slot, 1, :, lanes]
            tile = jnp.where(at_row == 0, before, jnp.where(at_row == 1, after, 0.0))
            return tile.astype(BF16)

        low, high = slice(0, rank), slice(rank, 2 * rank)
        factor_leaf[side, rows : rows + 16, :] = edge_tile(0, low)
        factor_leaf[1 - side, rows : rows + 16, :] = edge_tile(1, low)
        factor_middle[group, rows : rows + 16, :] = edge_tile(0, high)
        factor_middle[1 - group, rows : rows + 16, :] = edge_tile(2, high)

    leaf_base = LAG
    middle_at = leaf_base + (n_z - 1) * HOP + LAND + 1
    middle_base = middle_at + LAG
    top_at = middle_base + 2 + (n_z - 1) * HOP + LAND
    steps = top_at + 4 * (n_top - 1) + 1
    rank_leaf_now = rank_leaf[0]
    rank_middle_now = rank_middle[front // 2]

    def step(t, carry):
        @pl.when(t < n_leaf)
        def _():
            leaf_step(t)

        @pl.when(t == n_leaf)
        def _():
            ready()

        chain(
            t, n_leaf, leaf_base, 0, 1, leaf_lines, rank_leaf_now, coef_leaf, coef_leaf_sem,
            side, across,
        )

        i_mid = t - middle_at

        @pl.when(
            jnp.logical_and(i_mid >= 0, jnp.logical_and(i_mid < 2 * n_mid, lax.rem(i_mid, 2) == 0))
        )
        def _():
            middle_step(i_mid // 2)

        chain(
            t, n_mid, middle_base, n_leaf, 2, middle_lines, rank_middle_now, coef_middle, coef_middle_sem,
            group, over,
        )

        i_top = t - top_at

        @pl.when(jnp.logical_and(i_top >= 0, lax.rem(i_top, 4) == 0))
        def _():
            top_step(i_top // 4)

        return carry

    lax.fori_loop(0, steps, step, 0)

    @pl.when(sep < n_sep - 1)
    def _():
        for copy in to_next:
            copy.wait_send()

    @pl.when(sep > 0)
    def _():
        for copy in to_prev:
            copy.wait_send()

    for copy in factor_copies:
        copy.wait_send()

    def drain(lines, first_slot, j, carry):
        slot = first_slot + j
        pair_copy(slot).wait_send()

        @pl.when(z < n_z - 1)
        def _():
            right_copy(lines, first_slot, j).wait_send()

        @pl.when(z > 0)
        def _():
            left_copy(lines, first_slot, j).wait_send()

        final_copy(slot, coef_leaf, coef_leaf_sem, side, 0, front, sibling, 0).wait_send()

        @pl.when(lax.rem(j, 2) == 0)
        def _():
            final_copy(slot, coef_leaf, coef_leaf_sem, side, 0, across, sep, 1).wait_send()

        return carry

    lax.fori_loop(0, n_leaf, functools.partial(drain, leaf_lines, 0), 0)
    lax.fori_loop(0, n_mid, functools.partial(drain, middle_lines, n_leaf), 0)


def shards(*operands):
    n_sep = lax.axis_size("sep")
    rows, width = operands[0].shape[1:]
    rank = operands[3].shape[2]
    half, quarter = width // 2, width // 4
    own_rank = rank // 2
    n_top = quarter // CW
    n_mid = 2 * n_top
    slots = 3 * n_mid
    chunk = (slots, own_rank, CW)
    tail = width + half + quarter + 2 * CW
    dma = pltpu.SemaphoreType.DMA
    hbm = pl.BlockSpec(memory_space=pl.ANY)
    vmem = pl.BlockSpec(memory_space=pltpu.VMEM)
    smem = pl.BlockSpec(memory_space=pltpu.SMEM)
    return pl.pallas_call(
        functools.partial(kernel, n_sep),
        out_shape=jax.ShapeDtypeStruct((1, rows, quarter), F32),
        in_specs=[hbm] * 7 + [vmem] * 3 + [smem] * 3,
        out_specs=vmem,
        scratch_shapes=[
            pltpu.VMEM((rows, width), BF16),
            pltpu.VMEM((rows, half), BF16),
            pltpu.VMEM((rows, quarter), BF16),
            pltpu.VMEM((2, rows, rank), BF16),
            pltpu.VMEM((2, rows + 16, rank), BF16),
            pltpu.VMEM((2, rows + 16, rank), BF16),
            pltpu.VMEM((rank, rows), BF16),
            pltpu.VMEM((rank, rows), BF16),
            pltpu.VMEM((3, rows, CW), F32),
            pltpu.VMEM((2, 1, tail), F32),
            pltpu.VMEM((2, 1, tail), F32),
            pltpu.VMEM((2, 1, 2 * rank), F32),
            pltpu.VMEM((3, 2, 1, 2 * rank), F32),
            pltpu.VMEM(chunk, F32),
            pltpu.VMEM(chunk, F32),
            pltpu.VMEM(chunk, F32),
            pltpu.VMEM((4, 2 * n_mid, own_rank, CW), BF16),
            pltpu.VMEM((4, n_mid, own_rank, CW), F32),
            pltpu.VMEM(chunk, BF16),
            pltpu.VMEM((2, n_mid, rank, CW), BF16),
            pltpu.VMEM((2, n_top, rank, CW), BF16),
            dma((7,)),
            dma((2,)),
            dma((2,)),
            dma((2,)),
            dma((2,)),
            dma((3, 2)),
            dma((3, 2)),
            dma((slots,)),
            dma((slots,)),
            dma((slots,)),
            dma((slots,)),
            dma((slots,)),
            dma((slots,)),
            dma((slots, 2)),
            dma((n_mid, 3)),
            dma((n_top, 3)),
        ],
        compiler_params=pltpu.CompilerParams(
            collective_id=0, has_side_effects=True, vmem_limit_bytes=50 * 1024 * 1024
        ),
    )(*operands)


def solution(mesh):
    return jax.shard_map(
        shards,
        mesh=mesh,
        in_specs=(
            P("dom", "sep", None),
            P("dom", "sep", None),
            P("dom", "sep", None),
            P("dom", "sep", None),
            P("dom", "sep", None),
            P("dom", "sep", None),
            P("dom", "sep", None),
            P("dom", "sep"),
            P(None, "sep"),
            P(None, "sep"),
            P("dom", "sep"),
            P("dom"),
            P(),
        ),
        out_specs=P("dom", "sep", None),
        check_vma=False,
    )
```

time: 180 us -> 59.3 us (0.33); the launches traced: 177 us -> 58.9 us
  blocking collectives: 99.5 us -> 0 us
  Pallas kernels: 0 us -> 48 us
  waiting for transfers between devices: 46.7 us -> 0 us
  starting transfers between devices: 16.1 us -> 0 us
  matrix products: 7.85 us -> 0 us
  local copies, waits for them, and re-layouts: 2.12 us -> 9.5 us
  other arithmetic: 2.97 us -> 0 us
    psum x2 -> x0, blocking collectives: 99.5 us -> none  [coefficients(): return lax.psum(kept_sum, 'sep').astype(jnp.bfloat16)]
    pallas_call x0 -> x1, Pallas kernels: none -> 48 us  [shards(): pl.pallas_call(functools.partial(kernel, n_sep), out_shape=jax.ShapeDtype...]
    ppermute x8 -> x0, waiting for transfers between devices: 46.7 us -> none  [the longest x2 45.5 us: from_partner(): return lax.ppermute(value, axis, pairs)]
    ppermute x8 -> x0, starting transfers between devices: 16.1 us -> none  [the longest x3 9.1 us: extended(): lax.ppermute(tail, axis, [(i, (i + 1) % count) for i in range(ends)])]
    unnamed x17 -> x21, local copies, waits for them, and re-layouts: 0.25 us -> 9.5 us
    dot_general x6 -> x0, matrix products: 7.85 us -> none  [the longest x2 5.01 us: coefficients(): lax.dot_general(factor, values, (((0,), (0,)), ((), ())), preferred_eleme...]
  transfers between devices with their start and end apart: 8 -> 0, of which waited for: 5 -> 0; matrix products, arithmetic and copies ran while one was open for 1% -> 0% of each run, Pallas kernels for 0% -> 0%
where the time goes in v1:
time: 59.3 us; the launch traced here: 58.9 us
  Pallas kernels  48 us (81%)
  local copies, waits for them, and re-layouts  9.5 us (16%)
  between operations  1.32 us (2%)
    pallas_call x1, Pallas kernels, shards(): pl.pallas_call(functools.partial(kernel, n_sep), out_shape=jax.ShapeDtype...  48 us
    unnamed x21, local copies, waits for them, and re-layouts  9.5 us

profile of v1, /device:TPU:0, one launch (start us, length us, event | category | flops | bytes accessed | tf_op | source)
XLA Modules:
  0.0 58.9 jit_solution(15953068288986467034)
XLA Ops:
  1.3 0.0 copy-start
  1.3 1.1 %copy-done = bf16[1,512,768]{2,1,0:T(8,128)(2,1)S(1)} copy-done((bf16[1,512,768]{2,1,0:T(8,128)(2,1)S(1)}, bf16[1,512,768]{2,1,0:T(8,128)(2,1)}, u32[]{:S(2)}) %copy-start) | copy-done | bytes 786456
  2.4 0.0 copy-start.1
  2.4 1.0 %copy-done.1 = bf16[1,512,384]{2,1,0:T(8,128)(2,1)S(1)} copy-done((bf16[1,512,384]{2,1,0:T(8,128)(2,1)S(1)}, bf16[1,512,384]{2,1,0:T(8,128)(2,1)}, u32[]{:S(2)}) %copy-start.1) | copy-done | bytes 393240
  3.4 0.0 copy-start.2
  3.4 0.9 %copy-done.2 = bf16[1,512,256]{2,1,0:T(8,128)(2,1)S(1)} copy-done((bf16[1,512,256]{2,1,0:T(8,128)(2,1)S(1)}, bf16[1,512,256]{2,1,0:T(8,128)(2,1)}, u32[]{:S(2)}) %copy-start.2) | copy-done | bytes 262168
  4.4 0.0 copy-start.3
  4.4 0.9 %copy-done.3 = bf16[1,512,256]{2,1,0:T(8,128)(2,1)S(1)} copy-done((bf16[1,512,256]{2,1,0:T(8,128)(2,1)S(1)}, bf16[1,512,256]{2,1,0:T(8,128)(2,1)}, u32[]{:S(2)}) %copy-start.3) | copy-done | bytes 262168
  5.3 0.0 copy-start.4
  5.3 0.9 %copy-done.4 = bf16[1,512,256]{2,1,0:T(8,128)(2,1)S(1)} copy-done((bf16[1,512,256]{2,1,0:T(8,128)(2,1)S(1)}, bf16[1,512,256]{2,1,0:T(8,128)(2,1)}, u32[]{:S(2)}) %copy-start.4) | copy-done | bytes 262168
  6.3 0.0 copy-start.5
  6.3 0.9 %copy-done.5 = bf16[1,512,256]{2,1,0:T(8,128)(2,1)S(1)} copy-done((bf16[1,512,256]{2,1,0:T(8,128)(2,1)S(1)}, bf16[1,512,256]{2,1,0:T(8,128)(2,1)}, u32[]{:S(2)}) %copy-start.5) | copy-done | bytes 262168
  7.2 0.0 copy-start.6
  7.2 0.7 %copy-done.6 = f32[2,512]{1,0:T(2,128)S(1)} copy-done((f32[2,512]{1,0:T(2,128)S(1)}, f32[2,512]{1,0:T(2,128)}, u32[]{:S(2)}) %copy-start.6) | copy-done | bytes 4120
  7.9 0.0 copy-start.7
  7.9 0.7 %copy-done.7 = f32[1,512]{1,0:T(1,128)S(1)} copy-done((f32[1,512]{1,0:T(1,128)S(1)}, f32[1,512]{1,0:T(1,128)}, u32[]{:S(2)}) %copy-start.7) | copy-done | bytes 2072
  8.6 0.0 copy-start.8
  8.6 0.7 %copy-done.8 = f32[1,512]{1,0:T(1,128)S(1)} copy-done((f32[1,512]{1,0:T(1,128)S(1)}, f32[1,512]{1,0:T(1,128)}, u32[]{:S(2)}) %copy-start.8) | copy-done | bytes 2072
  9.3 0.0 copy-start.9
  9.3 0.7 %copy-done.9 = s32[2]{0:T(128)S(1)} copy-done((s32[2]{0:T(128)S(1)}, s32[2]{0:T(128)}, u32[]{:S(2)}) %copy-start.9) | copy-done | bytes 32
  9.9 48.0 %shard_map.127 = f32[1,512,384]{2,1,0:T(8,128)S(1)} custom-call(bf16[1,512,1536]{2,1,0:T(8,128)(2,1)} %rhs_leaf.1, bf16[1,512,768]{2,1,0:T(8,128)(2,1)S(1)} %copy-done, bf16[1,512,384]{2,1,0:T(8,128)(2,1)S(1)} %copy-done.1, bf16[1,512,256]{2,1,0:T(8,128)(2,1)S(1)} %copy-done.2, bf16[1,512,256]{2,1,0:T(8,128)(2,1)S(1)} %copy-done.3, ...), custom_call_target="tpu_custom_call" | custom-call | tf_op jit(solution)/shard_map/pallas_call | solution.py:506
  58.0 0.9 %copy.17 = f32[1,512,384]{2,1,0:T(8,128)} copy(f32[1,512,384]{2,1,0:T(8,128)S(1)} %shard_map.127) | data formatting | bytes 1572864
Async XLA Ops:
  1.3 1.1 %copy-start = (bf16[1,512,768]{2,1,0:T(8,128)(2,1)S(1)}, bf16[1,512,768]{2,1,0:T(8,128)(2,1)}, u32[]{:S(2)}) copy-start(bf16[1,512,768]{2,1,0:T(8,128)(2,1)} %rhs_middle.1) | copy-start | bytes 2359300
  2.4 1.0 %copy-start.1 = (bf16[1,512,384]{2,1,0:T(8,128)(2,1)S(1)}, bf16[1,512,384]{2,1,0:T(8,128)(2,1)}, u32[]{:S(2)}) copy-start(bf16[1,512,384]{2,1,0:T(8,128)(2,1)} %rhs_top.1) | copy-start | bytes 1179652
  3.4 0.9 %copy-start.2 = (bf16[1,512,256]{2,1,0:T(8,128)(2,1)S(1)}, bf16[1,512,256]{2,1,0:T(8,128)(2,1)}, u32[]{:S(2)}) copy-start(bf16[1,512,256]{2,1,0:T(8,128)(2,1)} %update_leaf.1) | copy-start | bytes 786436
  4.4 0.9 %copy-start.3 = (bf16[1,512,256]{2,1,0:T(8,128)(2,1)S(1)}, bf16[1,512,256]{2,1,0:T(8,128)(2,1)}, u32[]{:S(2)}) copy-start(bf16[1,512,256]{2,1,0:T(8,128)(2,1)} %couple_leaf.1) | copy-start | bytes 786436
  5.3 0.9 %copy-start.4 = (bf16[1,512,256]{2,1,0:T(8,128)(2,1)S(1)}, bf16[1,512,256]{2,1,0:T(8,128)(2,1)}, u32[]{:S(2)}) copy-start(bf16[1,512,256]{2,1,0:T(8,128)(2,1)} %update_middle.1) | copy-start | bytes 786436
  6.3 0.9 %copy-start.5 = (bf16[1,512,256]{2,1,0:T(8,128)(2,1)S(1)}, bf16[1,512,256]{2,1,0:T(8,128)(2,1)}, u32[]{:S(2)}) copy-start(bf16[1,512,256]{2,1,0:T(8,128)(2,1)} %couple_middle.1) | copy-start | bytes 786436
  7.2 0.7 %copy-start.6 = (f32[2,512]{1,0:T(2,128)S(1)}, f32[2,512]{1,0:T(2,128)}, u32[]{:S(2)}) copy-start(f32[2,512]{1,0:T(2,128)} %pivot_middle.1) | copy-start | bytes 12292
  7.9 0.7 %copy-start.7 = (f32[1,512]{1,0:T(1,128)S(1)}, f32[1,512]{1,0:T(1,128)}, u32[]{:S(2)}) copy-start(f32[1,512]{1,0:T(1,128)} %pivot_leaf.1) | copy-start | bytes 6148
  8.6 0.7 %copy-start.8 = (f32[1,512]{1,0:T(1,128)S(1)}, f32[1,512]{1,0:T(1,128)}, u32[]{:S(2)}) copy-start(f32[1,512]{1,0:T(1,128)} %pivot_top.1) | copy-start | bytes 6148
  9.3 0.7 %copy-start.9 = (s32[2]{0:T(128)S(1)}, s32[2]{0:T(128)}, u32[]{:S(2)}) copy-start(s32[2]{0:T(128)} %rank_middle.1) | copy-start | bytes 28

commit v2 on v1

--- a/solution.py
+++ b/solution.py
@@ -11,9 +11,9 @@
 F32 = jnp.float32
 BF16 = jnp.bfloat16
 CW = 128
-HOP = 3
-LAG = 2
-LAND = 2
+HOP = 5
+LAG = 3
+LAND = 4
 
 
 def flipped(value, bit):
@@ -29,6 +29,7 @@
     rhs_leaf, rhs_middle, rhs_top, update_leaf, couple_leaf, update_middle, couple_middle,
     pivot_leaf, pivot_middle, pivot_top, front_rows, rank_leaf, rank_middle,
     out,
+    pivot_v,
     leaf_v, middle_v, top_v, couple_v, factor_leaf, factor_middle,
     turned_leaf, turned_middle, weights,
     edge_send, edge_recv, row_send, row_recv,
@@ -65,6 +66,9 @@
     n_leaf = 2 * n_mid
 
     loads = [
+        pltpu.make_async_copy(pivot_leaf, pivot_v.at[0], load_sem.at[7]),
+        pltpu.make_async_copy(pivot_middle.at[pl.ds(front // 2, 1)], pivot_v.at[1], load_sem.at[8]),
+        pltpu.make_async_copy(pivot_top.at[pl.ds(front // 4, 1)], pivot_v.at[2], load_sem.at[9]),
         pltpu.make_async_copy(rhs_leaf.at[0], leaf_v, load_sem.at[0]),
         pltpu.make_async_copy(couple_leaf.at[0], couple_v.at[0], load_sem.at[1]),
         pltpu.make_async_copy(
@@ -127,11 +131,13 @@
 
     row_at = lax.broadcasted_iota(jnp.int32, (rows, CW), 0)
     live = (row_at < front_rows[0, 0]).astype(F32)
-    weights[0] = live * (1.0 / spread(pivot_leaf[...], CW))
-    weights[1] = 1.0 / spread(pivot_middle[pl.ds(front // 2, 1), :], CW)
-    weights[2] = 1.0 / spread(pivot_top[pl.ds(front // 4, 1), :], CW)
-
-    for load in loads[:6]:
+    for load in loads[:3]:
+        load.wait()
+    weights[0] = live * (1.0 / spread(pivot_v[0], CW))
+    weights[1] = 1.0 / spread(pivot_v[1], CW)
+    weights[2] = 1.0 / spread(pivot_v[2], CW)
+
+    for load in loads[3:9]:
         load.wait()
 
     ends = (rows - 16, 0)
@@ -224,7 +230,7 @@
     def place(i):
         here = lax.rem(i, 2)
         at_quarter = here * group + (1 - here) * (1 - group)
-        return at_quarter * n_top + i // 2
+        return at_quarter * n_top + lax.div(i, 2)
 
     def to_device(src, dst, send_sem, recv_sem, dom_at, sep_at):
         return pltpu.make_async_remote_copy(
@@ -266,10 +272,12 @@
 
     def chain(t, count, base, first_slot, stride, lines, rank_now, coef, coef_sem, child, partner):
         def on(step, body):
-            j = (step + stride * count) // stride - count
-            hit = jnp.logical_and(lax.rem(step + stride * count, stride) == 0, True)
-
-            @pl.when(jnp.logical_and(hit, jnp.logical_and(step >= 0, j < count)))
+            j = lax.div(step, stride) if stride > 1 else step
+            hit = jnp.logical_and(step >= 0, step < stride * count)
+            if stride > 1:
+                hit = jnp.logical_and(hit, lax.rem(step, stride) == 0)
+
+            @pl.when(hit)
             def _():
                 body(j)
 
@@ -308,7 +316,7 @@
             at = core * own_rank + lax.broadcasted_iota(jnp.int32, total.shape, 0)
             kept = jnp.where(at < rank_now, total, 0.0).astype(BF16)
             final_send[slot] = kept
-            i = j // 2
+            i = lax.div(j, 2)
 
             @pl.when(lax.rem(j, 2) == 1)
             def _():
@@ -339,7 +347,7 @@
         )
 
     def leaf_step(j):
-        i = j // 2
+        i = lax.div(j, 2)
         own_side = lax.rem(j, 2)
         at_side = own_side * side + (1 - own_side) * (1 - side)
         at = pl.multiple_of(at_side * half + place(i) * CW, CW)
@@ -376,7 +384,7 @@
         )
 
     def ready():
-        loads[6].wait()
+        loads[9].wait()
         turn(1, turned_middle)
 
         @pl.when(sep > 0)
@@ -423,10 +431,12 @@
         def _():
             ready()
 
-        chain(
-            t, n_leaf, leaf_base, 0, 1, leaf_lines, rank_leaf_now, coef_leaf, coef_leaf_sem,
-            side, across,
-        )
+        @pl.when(t < leaf_base + n_leaf + (n_z - 1) * HOP)
+        def _():
+            chain(
+                t, n_leaf, leaf_base, 0, 1, leaf_lines, rank_leaf_now, coef_leaf, coef_leaf_sem,
+                side, across,
+            )
 
         i_mid = t - middle_at
 
@@ -434,18 +444,20 @@
             jnp.logical_and(i_mid >= 0, jnp.logical_and(i_mid < 2 * n_mid, lax.rem(i_mid, 2) == 0))
         )
         def _():
-            middle_step(i_mid // 2)
-
-        chain(
-            t, n_mid, middle_base, n_leaf, 2, middle_lines, rank_middle_now, coef_middle, coef_middle_sem,
-            group, over,
-        )
+            middle_step(lax.div(i_mid, 2))
+
+        @pl.when(t >= middle_base)
+        def _():
+            chain(
+                t, n_mid, middle_base, n_leaf, 2, middle_lines, rank_middle_now, coef_middle,
+                coef_middle_sem, group, over,
+            )
 
         i_top = t - top_at
 
         @pl.when(jnp.logical_and(i_top >= 0, lax.rem(i_top, 4) == 0))
         def _():
-            top_step(i_top // 4)
+            top_step(lax.div(i_top, 4))
 
         return carry
 
@@ -500,15 +512,16 @@
     chunk = (slots, own_rank, CW)
     tail = width + half + quarter + 2 * CW
     dma = pltpu.SemaphoreType.DMA
-    hbm = pl.BlockSpec(memory_space=pl.ANY)
+    hbm = pl.BlockSpec(memory_space=pltpu.HBM)
     vmem = pl.BlockSpec(memory_space=pltpu.VMEM)
     smem = pl.BlockSpec(memory_space=pltpu.SMEM)
     return pl.pallas_call(
         functools.partial(kernel, n_sep),
         out_shape=jax.ShapeDtypeStruct((1, rows, quarter), F32),
-        in_specs=[hbm] * 7 + [vmem] * 3 + [smem] * 3,
+        in_specs=[hbm] * 10 + [smem] * 3,
         out_specs=vmem,
         scratch_shapes=[
+            pltpu.VMEM((3, 1, rows), F32),
             pltpu.VMEM((rows, width), BF16),
             pltpu.VMEM((rows, half), BF16),
             pltpu.VMEM((rows, quarter), BF16),
@@ -530,7 +543,7 @@
             pltpu.VMEM(chunk, BF16),
             pltpu.VMEM((2, n_mid, rank, CW), BF16),
             pltpu.VMEM((2, n_top, rank, CW), BF16),
-            dma((7,)),
+            dma((10,)),
             dma((2,)),
             dma((2,)),
             dma((2,)),
@@ -548,7 +561,7 @@
             dma((n_top, 3)),
         ],
         compiler_params=pltpu.CompilerParams(
-            collective_id=0, has_side_effects=True, vmem_limit_bytes=50 * 1024 * 1024
+            collective_id=0, has_side_effects=True, vmem_limit_bytes=67043328
         ),
     )(*operands)
 

time: 59.3 us -> 51.4 us (0.87)
  local copies, waits for them, and re-layouts: 9.5 us -> 2.06 us
    unnamed x21 -> x1, local copies, waits for them, and re-layouts: 9.5 us -> 2.06 us
where the time goes in v2:
time: 51.4 us; the launch traced here: 51.2 us
  Pallas kernels  47.9 us (93%)
  local copies, waits for them, and re-layouts  2.06 us (4%)
  between operations  1.3 us (3%)
    pallas_call x1, Pallas kernels, shards(): pl.pallas_call(functools.partial(kernel, n_sep), out_shape=jax.ShapeDtype...  47.9 us
    unnamed x1, local copies, waits for them, and re-layouts  2.06 us

profile of v2, /device:TPU:0, one launch (start us, length us, event | category | flops | bytes accessed | tf_op | source)
XLA Modules:
  0.0 51.2 jit_solution(4620789724980179736)
XLA Ops:
  1.3 47.9 %shard_map.127 = f32[1,512,384]{2,1,0:T(8,128)} custom-call(bf16[1,512,1536]{2,1,0:T(8,128)(2,1)} %rhs_leaf.1, bf16[1,512,768]{2,1,0:T(8,128)(2,1)} %rhs_middle.1, bf16[1,512,384]{2,1,0:T(8,128)(2,1)} %rhs_top.1, bf16[1,512,256]{2,1,0:T(8,128)(2,1)} %update_leaf.1, bf16[1,512,256]{2,1,0:T(8,128)(2,1)} %couple_leaf.1, bf16[1,512,256]{2,1,0:T(8,128)(2,1)} %update_middle.1, ...), custom_call_target="tpu_custom_call" | custom-call | tf_op jit(solution)/shard_map/pallas_call | solution.py:518
  49.2 2.1 %copy.17 = f32[1,512,384]{2,1,0:T(8,128)} copy(f32[1,512,384]{2,1,0:T(8,128)} %shard_map.127) | data formatting | bytes 1572864

commit v3 on v2

--- a/solution.py
+++ b/solution.py
@@ -27,9 +27,9 @@
 def kernel(
     n_sep,
     rhs_leaf, rhs_middle, rhs_top, update_leaf, couple_leaf, update_middle, couple_middle,
-    pivot_leaf, pivot_middle, pivot_top, front_rows, rank_leaf, rank_middle,
+    pivot_leaf, pivot_middle, pivot_top, front_rows_hbm, rank_leaf_hbm, rank_middle_hbm,
     out,
-    pivot_v,
+    front_rows, rank_leaf, rank_middle, pivot_v,
     leaf_v, middle_v, top_v, couple_v, factor_leaf, factor_middle,
     turned_leaf, turned_middle, weights,
     edge_send, edge_recv, row_send, row_recv,
@@ -66,6 +66,9 @@
     n_leaf = 2 * n_mid
 
     loads = [
+        pltpu.make_async_copy(front_rows_hbm, front_rows, load_sem.at[10]),
+        pltpu.make_async_copy(rank_leaf_hbm, rank_leaf, load_sem.at[11]),
+        pltpu.make_async_copy(rank_middle_hbm, rank_middle, load_sem.at[12]),
         pltpu.make_async_copy(pivot_leaf, pivot_v.at[0], load_sem.at[7]),
         pltpu.make_async_copy(pivot_middle.at[pl.ds(front // 2, 1)], pivot_v.at[1], load_sem.at[8]),
         pltpu.make_async_copy(pivot_top.at[pl.ds(front // 4, 1)], pivot_v.at[2], load_sem.at[9]),
@@ -129,15 +132,15 @@
         for lines in (leaf_lines, middle_lines):
             lines[3] = jnp.zeros(lines.shape[1:], lines.dtype)
 
+    for load in loads[:6]:
+        load.wait()
     row_at = lax.broadcasted_iota(jnp.int32, (rows, CW), 0)
     live = (row_at < front_rows[0, 0]).astype(F32)
-    for load in loads[:3]:
-        load.wait()
     weights[0] = live * (1.0 / spread(pivot_v[0], CW))
     weights[1] = 1.0 / spread(pivot_v[1], CW)
     weights[2] = 1.0 / spread(pivot_v[2], CW)
 
-    for load in loads[3:9]:
+    for load in loads[6:12]:
         load.wait()
 
     ends = (rows - 16, 0)
@@ -384,7 +387,7 @@
         )
 
     def ready():
-        loads[9].wait()
+        loads[12].wait()
         turn(1, turned_middle)
 
         @pl.when(sep > 0)
@@ -514,13 +517,15 @@
     dma = pltpu.SemaphoreType.DMA
     hbm = pl.BlockSpec(memory_space=pltpu.HBM)
     vmem = pl.BlockSpec(memory_space=pltpu.VMEM)
-    smem = pl.BlockSpec(memory_space=pltpu.SMEM)
     return pl.pallas_call(
         functools.partial(kernel, n_sep),
         out_shape=jax.ShapeDtypeStruct((1, rows, quarter), F32),
-        in_specs=[hbm] * 10 + [smem] * 3,
+        in_specs=[hbm] * 13,
         out_specs=vmem,
         scratch_shapes=[
+            pltpu.SMEM(operands[10].shape, jnp.int32),
+            pltpu.SMEM(operands[11].shape, jnp.int32),
+            pltpu.SMEM(operands[12].shape, jnp.int32),
             pltpu.VMEM((3, 1, rows), F32),
             pltpu.VMEM((rows, width), BF16),
             pltpu.VMEM((rows, half), BF16),
@@ -543,7 +548,7 @@
             pltpu.VMEM(chunk, BF16),
             pltpu.VMEM((2, n_mid, rank, CW), BF16),
             pltpu.VMEM((2, n_top, rank, CW), BF16),
-            dma((10,)),
+            dma((13,)),
             dma((2,)),
             dma((2,)),
             dma((2,)),

time: 51.4 us -> 50.9 us (level)
  Pallas kernels: 47.9 us -> 47.3 us
    pallas_call x1, Pallas kernels: 47.9 us -> 47.3 us  [shards(): pl.pallas_call(functools.partial(kernel, n_sep), out_shape=jax.ShapeDtype...]
where the time goes in v3:
time: 50.9 us; the launch traced here: 50.7 us
  Pallas kernels  47.3 us (93%)
  local copies, waits for them, and re-layouts  2.06 us (4%)
  between operations  1.3 us (3%)
    pallas_call x1, Pallas kernels, shards(): pl.pallas_call(functools.partial(kernel, n_sep), out_shape=jax.ShapeDtype...  47.3 us
    unnamed x1, local copies, waits for them, and re-layouts  2.06 us

profile of v3, /device:TPU:0, one launch (start us, length us, event | category | flops | bytes accessed | tf_op | source)
XLA Modules:
  0.0 50.7 jit_solution(1826644355205197867)
XLA Ops:
  1.3 47.3 %shard_map.127 = f32[1,512,384]{2,1,0:T(8,128)} custom-call(bf16[1,512,1536]{2,1,0:T(8,128)(2,1)} %rhs_leaf.1, bf16[1,512,768]{2,1,0:T(8,128)(2,1)} %rhs_middle.1, bf16[1,512,384]{2,1,0:T(8,128)(2,1)} %rhs_top.1, bf16[1,512,256]{2,1,0:T(8,128)(2,1)} %update_leaf.1, bf16[1,512,256]{2,1,0:T(8,128)(2,1)} %couple_leaf.1, bf16[1,512,256]{2,1,0:T(8,128)(2,1)} %update_middle.1, ...), custom_call_target="tpu_custom_call" | custom-call | tf_op jit(solution)/shard_map/pallas_call | solution.py:520
  48.6 2.1 %copy.17 = f32[1,512,384]{2,1,0:T(8,128)} copy(f32[1,512,384]{2,1,0:T(8,128)} %shard_map.127) | data formatting | bytes 1572864
